TPU v7x, 256 devices: a whole 4x4x8 slice. The times are simulated.
256 devices in a mesh: blk: 64 (over y_lo, x, z), states: 4 (over y_hi, core).
Axes of the slice: x: 4, y: 4 (y_hi: 2, y_lo: 2; y = y_hi * 2 + y_lo), z: 8, core: 2. Of those that a mesh axis runs over, the one named last changes fastest.
Arguments:
- start_states: float32 [128, 16, 128, 512], P('blk', None, None, 'states'), may hold values from -6 to 6
- couplings: float32 [16, 128, 128], replicated, may hold values from -0.1875 to 0.1875
- potential: float32 [128, 16, 128], P('blk'), may hold values from -18 to 18
- site_offsets: int32 [128, 6, 16], P('blk'), may hold values from 0 to 15
- coupling_index: int32 [128, 7, 16], P('blk'), may hold values from 0 to 15
- degrees: int32 [512], P('states'), may hold values from 1 to 3, as said below
Outputs:
- orthonormal: float32 [128, 16, 128, 512], P('blk', 'states')
Inputs may be any that keep to these rules, and one draw needn't show every extreme that they name: `degrees`: every degree from 1 to 3 belongs to some state.
All inputs are finite; a program needn't handle non-finite values.
Results may differ from a plain program's by a relative error of at most 0.0003.
Values sent between devices are 32-bit elements; how exact they have to be, the bound alone decides.
A program may use at most 128 MiB of HBM per device.

v0:
```python
import jax
import jax.numpy as jnp
from jax import lax
from jax.sharding import PartitionSpec as P

cut_share = 0.3
exact = lax.Precision.HIGHEST


def padded_2(shard, sides, width):
    for axis, dim in sides:
        devices, length = (lax.axis_size(axis), shard.shape[dim])
        up = [(i, (i + 1) % devices) for i in range(devices)]
        down = [(j, i) for i, j in up]
        last = lax.slice_in_dim(shard, length - width, length, axis=dim)
        first = lax.slice_in_dim(shard, 0, width, axis=dim)
        before = lax.ppermute(last, axis, up)
        after = lax.ppermute(first, axis, down)
        shard = jnp.concatenate([before, shard, after], axis=dim)
    return shard


def copy_for_each(shard, axis):
    copies = jnp.broadcast_to(shard, (lax.axis_size(axis), *shard.shape))
    return lax.all_to_all(copies, axis, split_axis=0, concat_axis=0, tiled=True)


def folded_in_pairs(pieces, combine):
    while len(jax.tree.leaves(pieces)[0]) > 1:
        pieces = jax.vmap(combine)(
            *(jax.tree.map(lambda part: part[side::2], pieces) for side in (0, 1))
        )
    return jax.tree.map(lambda part: part[0], pieces)


def joined_all(shard, axis, combine):
    pieces = jax.tree.map(lambda part: copy_for_each(part, axis), shard)
    return folded_in_pairs(pieces, combine)


def coupling_blocks(couplings, index_rows):
    return jnp.take(couplings, index_rows, axis=0)


def apply_inner(padded, blocks_used, onsite, offset_rows):
    middle = padded[1:-1]
    lower_layers = padded[:-2]
    upper_layers = padded[2:]
    count = onsite.shape[1]
    site_ids = jnp.arange(count, dtype=jnp.int32)
    layer_ids = jnp.arange(middle.shape[0], dtype=jnp.int32)
    pieces = [middle]
    for slot in range(1, 7):
        if slot == 5:
            source = lower_layers
        elif slot == 6:
            source = upper_layers
        else:
            source = middle
        neighbour = (site_ids[None, :] + offset_rows[:, slot - 1, :]) % count
        pieces.append(source[layer_ids[:, None], neighbour])
    stacked = jnp.stack(pieces, axis=1)
    summed = jnp.einsum("lksij,lksjn->lsin", blocks_used, stacked, precision=exact)
    return summed + onsite[..., None] * middle


def extrema_of(couplings, onsite, index_rows):
    row_abs = jnp.sum(jnp.abs(couplings), axis=2)
    diag_all = jnp.diagonal(couplings, axis1=1, axis2=2)
    table_ids = jnp.arange(couplings.shape[0], dtype=jnp.int32)
    onehot = (index_rows[..., None] == table_ids).astype(jnp.float32)
    picked_abs = jnp.einsum("lksc,ci->lksi", onehot, row_abs, precision=exact)
    picked_diag = jnp.einsum("lsc,ci->lsi", onehot[:, 0], diag_all, precision=exact)
    centers = picked_diag + onsite
    radii = picked_abs[:, 0] - jnp.abs(picked_diag) + jnp.sum(picked_abs[:, 1:], axis=1)
    return (jnp.max(centers + radii), jnp.min(centers - radii))


def combine(first, second):
    return (jnp.maximum(first[0], second[0]), jnp.minimum(first[1], second[1]))


def faces(field):
    return padded_2(field, (("blk", 0),), 1)


def per_device(start_states, couplings, potential, site_offsets, coupling_index, degrees):
    upper, lower = joined_all(extrema_of(couplings, potential, coupling_index), "blk", combine)
    cut_edge = lower + cut_share * (upper - lower)
    middle_value = (upper + cut_edge) / 2.0
    half_width = (upper - cut_edge) / 2.0

    def scaled(applied, field):
        return (applied - middle_value * field) / half_width

    local_blocks = coupling_blocks(couplings, coupling_index)
    first_step = scaled(
        apply_inner(faces(start_states), local_blocks, potential, site_offsets), start_states
    )
    second = (
        2.0
        * scaled(apply_inner(faces(first_step), local_blocks, potential, site_offsets), first_step)
        - start_states
    )
    third = (
        2.0 * scaled(apply_inner(faces(second), local_blocks, potential, site_offsets), second)
        - first_step
    )
    chosen = jnp.where(degrees == 1, first_step, jnp.where(degrees == 2, second, third))
    regrouped = lax.all_to_all(chosen, "states", split_axis=1, concat_axis=3, tiled=True)
    rows = regrouped.reshape(-1, regrouped.shape[-1])
    partial_gram = lax.dot_general(
        rows, rows, (((0,), (0,)), ((), ())), precision=exact, preferred_element_type=jnp.float32
    )
    gram = lax.psum(partial_gram, ("blk", "states"))
    factor = jnp.linalg.cholesky(gram)
    identity = jnp.eye(gram.shape[0], dtype=jnp.float32)
    inverse_factor = jax.scipy.linalg.solve_triangular(factor, identity, lower=True)
    orthonormal = jnp.dot(
        rows, inverse_factor.T, precision=exact, preferred_element_type=jnp.float32
    )
    return orthonormal.reshape(regrouped.shape)


def solution(mesh):
    in_specs = (
        P("blk", None, None, "states"),
        P(),
        P("blk", None, None),
        P("blk", None, None),
        P("blk", None, None),
        P("states"),
    )
    out_specs = P("blk", "states", None, None)
    return jax.shard_map(
        per_device, mesh=mesh, in_specs=in_specs, out_specs=out_specs, check_vma=False
    )
```

profile of v0, /device:TPU:2, one launch (start us, length us, event | category | flops | bytes accessed | tf_op | source)
XLA Modules:
  0.0 722.4 jit_solution(9385407167922655574)
XLA Ops:
  8.1 6.1 copy.46
  18.6 13.0 %all-to-all-start = ((f32[64,1,1]{2,1,0:T(1,128)}), f32[64,1,1]{2,1,0:T(1,128)S(1)}, u32[]{:S(2)}, u32[]{:S(2)}) async-start(f32[64,1,1]{2,1,0:T(1,128)} %broadcast_in_dim.49), calls=%async_computation | async-start | bytes 65536 | tf_op jit(solution)/shard_map/all_to_all | solution.py:25
  33.2 2.7 collective-permute-start.1
  45.9 3.4 constant_dynamic-update-slice_fusion.5
  55.6 6.7 gather_fusion
  63.7 12.0 %all-to-all-start.1 = ((f32[64,1,1]{2,1,0:T(1,128)}), f32[64,1,1]{2,1,0:T(1,128)S(1)}, u32[]{:S(2)}, u32[]{:S(2)}) async-start(f32[64,1,1]{2,1,0:T(1,128)} %broadcast_in_dim.50), calls=%async_computation.1 | async-start | bytes 65536 | tf_op jit(solution)/shard_map/all_to_all | solution.py:25
  77.5 7.6 %all-to-all-done.1 = f32[64,1,1]{2,1,0:T(1,128)S(1)} async-done(((f32[64,1,1]{2,1,0:T(1,128)}), f32[64,1,1]{2,1,0:T(1,128)S(1)}, u32[]{:S(2)}, u32[]{:S(2)}) %all-to-all-start.1) | async-done | bytes 288 | tf_op jit(solution)/shard_map/all_to_all | solution.py:25
  90.6 4.1 pad_maximum_fusion.4
  94.7 3.6 gather_fusion.5
  98.3 3.1 constant_dynamic-update-slice_fusion.1
  101.4 3.6 gather_fusion.6
  105.0 3.1 constant_dynamic-update-slice_fusion
  108.1 21.0 %bitcast_dynamic-update-slice_fusion.2 = (f32[2,7,16,128,128]{4,3,2,0,1:T(8,128)}, f32[2,16,128,128]{3,2,1,0:T(8,128)S(1)}) fusion(f32[]{:T(128)S(6)} %div.29, f32[2,16,128,128]{3,2,1,0:T(8,128)S(1)} %copy-done.1, f32[]{:T(128)S(6)} %div.28, f32[2,16,128]{2,1,0:T(8,128)S(1)} %copy-done.22, f32[2,7,16,128,128]{4,3,1,2,0:T(8,128)} %constant_dynamic-update-slice_fusion, ...), kind=kOutput, calls=%fused_computation.56 | convolution fusion | flops 5643436032 | bytes 35668200 | tf_op jit(solution)/shard_map/lksij,lksjn->lsin/dot_general | solution.py:63
  133.6 3.6 gather_fusion.8
  137.2 3.6 gather_fusion.9
  140.8 3.6 gather_fusion.10
  144.4 3.6 gather_fusion.11
  148.0 3.3 constant_dynamic-update-slice_fusion.11
  158.3 3.6 pad_maximum_fusion.2
  161.9 3.6 gather_fusion.12
  165.5 3.6 gather_fusion.13
  169.1 3.3 constant_dynamic-update-slice_fusion.7
  173.9 21.6 %bitcast_dynamic-update-slice_fusion.1 = (f32[2,7,16,128,128]{4,3,2,0,1:T(8,128)}, f32[2,16,128,128]{3,2,1,0:T(8,128)}) fusion(f32[2,16,128,128]{3,2,1,0:T(8,128)S(1)} %copy-done.1, f32[]{:T(128)S(6)} %div.29, f32[2,16,128,128]{3,2,1,0:T(8,128)} %copy-done.2, f32[]{:T(128)S(6)} %div.28, f32[2,16,128]{2,1,0:T(8,128)S(1)} %copy-done.22, ...), kind=kOutput, calls=%fused_computation.50 | convolution fusion | flops 5644484608 | bytes 37765352 | tf_op jit(solution)/shard_map/lksij,lksjn->lsin/dot_general | solution.py:63
  195.5 2.9 fusion.105
  198.4 3.8 collective-permute-start.5
  210.5 3.3 constant_dynamic-update-slice_fusion.17
  221.8 4.3 collective-permute-done.4
  226.0 4.0 pad_maximum_fusion
  232.3 3.6 gather_fusion.19
  241.2 21.2 %fusion.19 = f32[2,16,128,128]{3,2,1,0:T(8,128)} fusion(f32[2,16,128,128]{3,2,1,0:T(8,128)S(1)} %copy-done.4, f32[2,16,128,128]{3,2,1,0:T(8,128)S(1)} %copy-done.6, f32[2,7,16,128,128]{4,3,2,0,1:T(8,128)} %constant_dynamic-update-slice_fusion.12, f32[2,7,16,128,128]{4,3,2,1,0:T(8,128)} %bitcast.190, pred[2,7,16]{1,2,0:T(8,128)(4,1)S(1)} %copy.43, ...), kind=kOutput, calls=%fused_computation.49 | convolution fusion | flops 5645533184 | bytes 35668456 | tf_op jit(solution)/shard_map/lksij,lksjn->lsin/dot_general | solution.py:63
  264.2 31.1 %all_to_all.33 = f32[2,16,128,128]{3,2,0,1:T(8,128)S(1)} all-to-all(f32[2,16,128,128]{3,2,0,1:T(8,128)S(1)} %copy.52), channel_id=1, replica_groups=mesh['blk'=64,'states'=4] {'states'}, dimensions={1} | all-to-all | bytes 4194304 | tf_op jit(solution)/shard_map/all_to_all | solution.py:110
  296.7 4.5 fusion.11
  305.6 250.9 %all-reduce.3.cloned.1.call-done = f32[512,512]{0,1:T(8,128)} async-done(((f32[512,512]{0,1:T(8,128)}), f32[512,512]{0,1:T(8,128)}) %all-reduce.3.cloned.1.call-update) | async-done | bytes 1048592 | tf_op jit(solution)/shard_map/psum | solution.py:115
  556.5 2.6 copy.55
  561.6 11.7 %cholesky.104 = f32[128,128]{1,0:T(8,128)S(1)} custom-call(f32[128,128]{1,0:T(8,128)S(1)} %cholesky.266), custom_call_target="Cholesky" | custom-call | tf_op jit(solution)/shard_map/jit(cholesky)/cholesky | solution.py:116
  573.5 9.8 %custom-call.31 = f32[1,128,128]{1,2,0:T(8,128)S(1)} custom-call(f32[1,128,128]{2,1,0:T(8,128)S(1)} %get-tuple-element.48), custom_call_target="InvertDiagBlocksLowerTriangular" | custom-call | tf_op jit(solution)/shard_map/jit(cholesky)/cholesky | solution.py:116
  585.8 11.7 %cholesky.217 = f32[128,128]{1,0:T(8,128)S(1)} custom-call(f32[128,128]{1,0:T(8,128)S(1)} %cholesky.270), custom_call_target="Cholesky" | custom-call | tf_op jit(solution)/shard_map/jit(cholesky)/cholesky | solution.py:116
  597.5 10.0 %custom-call.32 = f32[1,128,128]{1,2,0:T(8,128)S(1)} custom-call(f32[1,128,128]{2,1,0:T(8,128)S(1)} %get-tuple-element.45), custom_call_target="InvertDiagBlocksLowerTriangular" | custom-call | tf_op jit(solution)/shard_map/jit(cholesky)/cholesky | solution.py:116
  609.1 11.7 %cholesky.238 = f32[128,128]{1,0:T(8,128)S(1)} custom-call(f32[128,128]{1,0:T(8,128)S(1)} %cholesky.275), custom_call_target="Cholesky" | custom-call | tf_op jit(solution)/shard_map/jit(cholesky)/cholesky | solution.py:116
  620.8 9.8 %custom-call.33 = f32[1,128,128]{1,2,0:T(8,128)S(1)} custom-call(f32[1,128,128]{2,1,0:T(8,128)S(1)} %get-tuple-element.42), custom_call_target="InvertDiagBlocksLowerTriangular" | custom-call | tf_op jit(solution)/shard_map/jit(cholesky)/cholesky | solution.py:116
  632.1 11.7 %cholesky.255 = f32[128,128]{1,0:T(8,128)S(1)} custom-call(f32[128,128]{1,0:T(8,128)S(1)} %convolution_subtract_fusion.5), custom_call_target="Cholesky" | custom-call | tf_op jit(solution)/shard_map/jit(cholesky)/cholesky | solution.py:116
  649.7 13.9 %while.1 = (s32[]{:T(128)}, f32[512,512]{1,0:T(8,128)}, s32[4,2]{0,1:T(2,128)S(1)}, f32[4,128,128]{2,1,0:T(8,128)}, s32[]{:T(128)}) while((s32[]{:T(128)}, f32[512,512]{1,0:T(8,128)}, s32[4,2]{0,1:T(2,128)S(1)}, f32[4,128,128]{2,1,0:T(8,128)}, s32[]{:T(128)}) %tuple.46), condition=%wide.while_cond, body=%wide.while_body.sunk | while | flops 2 | bytes 132205 | solution.py:118
  650.4 2.9 bitcast_dynamic-update-slice_fusion.5
  653.9 2.9 bitcast_dynamic-update-slice_fusion.5
  657.4 2.9 bitcast_dynamic-update-slice_fusion.5
  660.9 2.8 bitcast_dynamic-update-slice_fusion.5
  663.7 40.1 %custom-call.34 = f32[4,128,128]{1,2,0:T(8,128)S(1)} custom-call(f32[4,128,128]{2,1,0:T(8,128)} %get-tuple-element.12), custom_call_target="InvertDiagBlocksLowerTriangular" | custom-call | tf_op jit(solution)/shard_map/jit(_solve_triangular)/triangular_solve | solution.py:118
  710.5 4.8 fusion.30
  (187 shorter events, 94.9 us)
Async XLA Ops:
  8.1 6.2 copy-start.23
  8.1 8.3 %copy-start.22 = (f32[2,16,128]{2,1,0:T(8,128)S(1)}, f32[2,16,128]{2,1,0:T(8,128)}, u32[]{:S(2)}) copy-start(f32[2,16,128]{2,1,0:T(8,128)} %param.8) | copy-start | bytes 49156
  8.1 23.5 %copy-start.1 = (f32[2,16,128,128]{3,2,1,0:T(8,128)S(1)}, f32[2,16,128,128]{3,2,1,0:T(8,128)}, u32[]{:S(2)}) copy-start(f32[2,16,128,128]{3,2,1,0:T(8,128)} %param.6) | copy-start | bytes 6291460
  18.6 43.8 %all-to-all-start = ((f32[64,1,1]{2,1,0:T(1,128)}), f32[64,1,1]{2,1,0:T(1,128)S(1)}, u32[]{:S(2)}, u32[]{:S(2)}) async-start(f32[64,1,1]{2,1,0:T(1,128)} %broadcast_in_dim.49), calls=%async_computation | async-start | bytes 65536 | tf_op jit(solution)/shard_map/all_to_all | solution.py:25
  33.2 57.4 %collective-permute-start.1 = (f32[1,16,128,128]{3,2,1,0:T(8,128)}, f32[1,16,128,128]{3,2,1,0:T(8,128)}, u32[]{:S(2)}, u32[]{:S(2)}) collective-permute-start(f32[1,16,128,128]{3,2,1,0:T(8,128)} %get-tuple-element.37), channel_id=1, source_target_pairs={{4,0},{8,4},{12,8},{16,12},{20,16},{24,20},{28,24},{32,28},{36,32}... | collective-permute-start | bytes 3145736 | tf_op jit(solution)/shard_map/ppermute | solution.py:18
  35.9 1.5 copy-start.24
  35.9 54.7 %collective-permute-start = (f32[1,16,128,128]{3,2,1,0:T(8,128)}, f32[1,16,128,128]{3,2,1,0:T(8,128)}, u32[]{:S(2)}, u32[]{:S(2)}) collective-permute-start(f32[1,16,128,128]{3,2,1,0:T(8,128)} %get-tuple-element.38), channel_id=1, source_target_pairs={{0,4},{4,8},{8,12},{12,16},{16,20},{20,24},{24,28},{28,32},{32,36}... | collective-permute-start | bytes 3145736 | tf_op jit(solution)/shard_map/ppermute | solution.py:17
  45.9 3.4 copy-start.8
  49.3 2.3 copy-start.9
  51.6 2.3 copy-start.10
  54.0 1.6 copy-start
  63.7 21.4 %all-to-all-start.1 = ((f32[64,1,1]{2,1,0:T(1,128)}), f32[64,1,1]{2,1,0:T(1,128)S(1)}, u32[]{:S(2)}, u32[]{:S(2)}) async-start(f32[64,1,1]{2,1,0:T(1,128)} %broadcast_in_dim.50), calls=%async_computation.1 | async-start | bytes 65536 | tf_op jit(solution)/shard_map/all_to_all | solution.py:25
  75.6 480.9 %all-reduce.3.cloned.1.call-start = ((), (), s32[]{:S(2)}) async-start(), calls=%async_computation.3 | async-start | bytes 2097152 | tf_op jit(solution)/shard_map/psum | solution.py:115
  129.2 2.0 copy-start.2
  131.2 26.2 %collective-permute-start.3 = (f32[1,16,128,128]{3,2,1,0:T(8,128)}, f32[1,16,128,128]{3,2,1,0:T(8,128)S(1)}, u32[]{:S(2)}, u32[]{:S(2)}) collective-permute-start(f32[1,16,128,128]{3,2,1,0:T(8,128)} %get-tuple-element.33), channel_id=1, source_target_pairs={{4,0},{8,4},{12,8},{16,12},{20,16},{24,20},{28,24},{32,28},{36,32}... | collective-permute-start | bytes 3145736 | tf_op jit(solution)/shard_map/ppermute | solution.py:18
  132.9 24.9 %collective-permute-start.2 = (f32[1,16,128,128]{3,2,1,0:T(8,128)}, f32[1,16,128,128]{3,2,1,0:T(8,128)}, u32[]{:S(2)}, u32[]{:S(2)}) collective-permute-start(f32[1,16,128,128]{3,2,1,0:T(8,128)} %get-tuple-element.34), channel_id=1, source_target_pairs={{0,4},{4,8},{8,12},{12,16},{16,20},{20,24},{24,28},{28,32},{32,36}... | collective-permute-start | bytes 3145736 | tf_op jit(solution)/shard_map/ppermute | solution.py:17
  148.0 3.3 copy-start.16
  151.2 2.3 copy-start.15
  153.6 2.3 copy-start.12
  155.9 2.3 copy-start.3
  169.0 3.3 copy-start.18
  195.5 6.8 copy-start.25
  195.5 6.8 copy-start.5
  198.4 23.4 %collective-permute-start.5 = (f32[1,16,128,128]{3,2,1,0:T(8,128)}, f32[1,16,128,128]{3,2,1,0:T(8,128)}, u32[]{:S(2)}, u32[]{:S(2)}) collective-permute-start(f32[1,16,128,128]{3,2,1,0:T(8,128)} %get-tuple-element.29), channel_id=1, source_target_pairs={{4,0},{8,4},{12,8},{16,12},{20,16},{24,20},{28,24},{32,28},{36,32}... | collective-permute-start | bytes 3145736 | tf_op jit(solution)/shard_map/ppermute | solution.py:18
  202.2 23.9 %collective-permute-start.4 = (f32[1,16,128,128]{3,2,1,0:T(8,128)S(1)}, f32[1,16,128,128]{3,2,1,0:T(8,128)}, u32[]{:S(2)}, u32[]{:S(2)}) collective-permute-start(f32[1,16,128,128]{3,2,1,0:T(8,128)S(1)} %get-tuple-element.30), channel_id=1, source_target_pairs={{0,4},{4,8},{8,12},{12,16},{16,20},{20,24},{24,28},{28,32},{32,36}... | collective-permute-start | bytes 3145736 | tf_op jit(solution)/shard_map/ppermute | solution.py:17
  210.5 3.3 copy-start.14
  213.8 2.3 copy-start.13
  216.1 2.3 copy-start.11
  235.9 2.3 copy-start.17
  238.2 2.3 copy-start.4
  238.2 3.0 copy-start.6
  296.7 4.5 copy-start.7
  556.5 2.6 copy-start.19
  560.6 1.0 copy-start.21
  649.7 57.0 %copy-start.20 = (f32[512,512]{1,0:T(8,128)S(1)}, f32[512,512]{1,0:T(8,128)}, u32[]{:S(2)}) copy-start(f32[512,512]{1,0:T(8,128)} %fusion.46) | copy-start | bytes 3145732
Sparse Core Ops, SparseCore 0:
  301.3 255.1 all-reduce.2
where the time goes:
time: 730 us; the launch traced here: 722 us
  waiting for transfers between devices  265 us (36%)
  local copies, waits for them, and re-layouts  148 us (20%)
  other arithmetic  138 us (19%)
  matrix products  86.3 us (12%)
  starting transfers between devices  34.2 us (5%)
  blocking collectives  31.1 us (4%)
  between operations  19.3 us (3%)
    psum x1, waiting for transfers between devices, per_device(): gram = lax.psum(partial_gram, ('blk', 'states'))  251 us
    another operation x14, other arithmetic, per_device(): factor = jnp.linalg.cholesky(gram)  78.6 us
    dot_general x3, matrix products, apply_inner(): jnp.einsum('lksij,lksjn->lsin', blocks_used, stacked, precision=exact)  63.8 us
    gather x18, local copies, waits for them, and re-layouts, apply_inner(): pieces.append(source[layer_ids[:, None], neighbour])  50.7 us
    unnamed x69, local copies, waits for them, and re-layouts  48.1 us
    another operation x3, other arithmetic, per_device(): jax.scipy.linalg.solve_triangular(factor, identity, lower=True)  41.4 us
    all_to_all x1, blocking collectives, per_device(): lax.all_to_all(chosen, 'states', split_axis=1, concat_axis=3, tiled=True)  31.1 us
    all_to_all x2, starting transfers between devices, copy_for_each(): return lax.all_to_all(copies, axis, split_axis=0, concat_axis=0, tiled=True)  25 us
  transfers between devices with their start and end apart: 9, of which 5 were waited for; matrix products, arithmetic and copies ran while one was open for 10% of the time, Pallas kernels for 0%

commit v1 on v0

--- a/solution.py
+++ b/solution.py
@@ -112,7 +112,8 @@
     partial_gram = lax.dot_general(
         rows, rows, (((0,), (0,)), ((), ())), precision=exact, preferred_element_type=jnp.float32
     )
-    gram = lax.psum(partial_gram, ("blk", "states"))
+    w1 = jax.lax.psum(partial_gram, "states")
+    gram = jax.lax.psum(w1, "blk")
     factor = jnp.linalg.cholesky(gram)
     identity = jnp.eye(gram.shape[0], dtype=jnp.float32)
     inverse_factor = jax.scipy.linalg.solve_triangular(factor, identity, lower=True)

time: 730 us -> 1140 us (1.56); the launches traced: 722 us -> 1120 us
  waiting for transfers between devices: 265 us -> 660 us
    psum x1 -> x2, waiting for transfers between devices: 251 us -> 646 us  [the longest x1 599 us: per_device(): gram = jax.lax.psum(w1, 'blk')]
    unnamed x69 -> x65, local copies, waits for them, and re-layouts: 48.1 us -> 48.4 us
  transfers between devices with their start and end apart: 9 -> 10, of which waited for: 5 -> 6; matrix products, arithmetic and copies ran while one was open for 10% -> 7% of each run, Pallas kernels for 0% -> 0%
where the time goes in v1:
time: 1140 us; the launch traced here: 1120 us
  waiting for transfers between devices  660 us (58%)
  local copies, waits for them, and re-layouts  151 us (13%)
  other arithmetic  138 us (12%)
  matrix products  86.8 us (8%)
  starting transfers between devices  34.3 us (3%)
  blocking collectives  31.1 us (3%)
  between operations  19.1 us (2%)
    psum x1, waiting for transfers between devices, per_device(): gram = jax.lax.psum(w1, 'blk')  599 us
    another operation x14, other arithmetic, per_device(): factor = jnp.linalg.cholesky(gram)  78.6 us
    dot_general x3, matrix products, apply_inner(): jnp.einsum('lksij,lksjn->lsin', blocks_used, stacked, precision=exact)  64.3 us
    gather x18, local copies, waits for them, and re-layouts, apply_inner(): pieces.append(source[layer_ids[:, None], neighbour])  52 us
    unnamed x65, local copies, waits for them, and re-layouts  48.4 us
    psum x1, waiting for transfers between devices, per_device(): w1 = jax.lax.psum(partial_gram, 'states')  46.5 us
    another operation x3, other arithmetic, per_device(): jax.scipy.linalg.solve_triangular(factor, identity, lower=True)  41.4 us
    all_to_all x1, blocking collectives, per_device(): lax.all_to_all(chosen, 'states', split_axis=1, concat_axis=3, tiled=True)  31.1 us
  transfers between devices with their start and end apart: 10, of which 6 were waited for; matrix products, arithmetic and copies ran while one was open for 7% of the time, Pallas kernels for 0%

profile of v1, /device:TPU:2, one launch (start us, length us, event | category | flops | bytes accessed | tf_op | source)
XLA Modules:
  0.0 1120.6 jit_solution(2403717683977411480)
XLA Ops:
  8.1 6.1 copy.46
  18.6 13.0 %all-to-all-start = ((f32[64,1,1]{2,1,0:T(1,128)}), f32[64,1,1]{2,1,0:T(1,128)S(1)}, u32[]{:S(2)}, u32[]{:S(2)}) async-start(f32[64,1,1]{2,1,0:T(1,128)} %broadcast_in_dim.49), calls=%async_computation | async-start | bytes 65536 | tf_op jit(solution)/shard_map/all_to_all | solution.py:25
  45.8 3.3 constant_dynamic-update-slice_fusion.5
  55.5 6.7 gather_fusion
  63.5 12.0 %all-to-all-start.1 = ((f32[64,1,1]{2,1,0:T(1,128)}), f32[64,1,1]{2,1,0:T(1,128)S(1)}, u32[]{:S(2)}, u32[]{:S(2)}) async-start(f32[64,1,1]{2,1,0:T(1,128)} %broadcast_in_dim.50), calls=%async_computation.1 | async-start | bytes 65536 | tf_op jit(solution)/shard_map/all_to_all | solution.py:25
  77.4 7.6 all-to-all-done.1
  90.3 3.9 pad_maximum_fusion.4
  94.2 3.6 gather_fusion.5
  97.8 3.1 constant_dynamic-update-slice_fusion.1
  100.9 3.6 gather_fusion.6
  104.5 3.1 constant_dynamic-update-slice_fusion
  107.7 21.4 %bitcast_dynamic-update-slice_fusion.2 = (f32[2,7,16,128,128]{4,3,2,0,1:T(8,128)}, f32[2,16,128,128]{3,2,1,0:T(8,128)}) fusion(f32[]{:T(128)S(6)} %div.29, f32[2,16,128,128]{3,2,1,0:T(8,128)S(1)} %copy-done.1, f32[]{:T(128)S(6)} %div.28, f32[2,16,128]{2,1,0:T(8,128)S(1)} %copy-done.20, f32[2,7,16,128,128]{4,3,1,2,0:T(8,128)} %constant_dynamic-update-slice_fusion, ...), kind=kOutput, calls=%fused_computation.56 | convolution fusion | flops 5643436032 | bytes 35668200 | tf_op jit(solution)/shard_map/lksij,lksjn->lsin/dot_general | solution.py:63
  134.3 3.6 gather_fusion.8
  137.9 3.6 gather_fusion.9
  141.5 3.6 gather_fusion.10
  145.1 3.6 gather_fusion.11
  148.6 3.3 constant_dynamic-update-slice_fusion.11
  158.9 4.0 pad_maximum_fusion.2
  163.0 3.6 gather_fusion.12
  166.6 3.6 gather_fusion.13
  170.1 3.3 constant_dynamic-update-slice_fusion.7
  175.0 21.6 %bitcast_dynamic-update-slice_fusion.1 = (f32[2,7,16,128,128]{4,3,2,0,1:T(8,128)}, f32[2,16,128,128]{3,2,1,0:T(8,128)}) fusion(f32[2,16,128,128]{3,2,1,0:T(8,128)S(1)} %copy-done.1, f32[]{:T(128)S(6)} %div.29, f32[2,16,128,128]{3,2,1,0:T(8,128)} %get-tuple-element.62, f32[]{:T(128)S(6)} %div.28, f32[2,16,128]{2,1,0:T(8,128)S(1)} %copy-done.20, ...), kind=kOutput, calls=%fused_computation.50 | convolution fusion | flops 5644484608 | bytes 37765352 | tf_op jit(solution)/shard_map/lksij,lksjn->lsin/dot_general | solution.py:63
  196.6 3.2 fusion.105
  199.8 3.8 collective-permute-start.5
  211.9 3.3 constant_dynamic-update-slice_fusion.17
  223.3 4.5 collective-permute-done.4
  227.7 4.0 pad_maximum_fusion
  231.7 3.6 gather_fusion.18
  235.3 3.6 gather_fusion.19
  238.9 3.3 constant_dynamic-update-slice_fusion.13
  244.6 21.2 %fusion.19 = f32[2,16,128,128]{3,2,1,0:T(8,128)} fusion(f32[2,16,128,128]{3,2,1,0:T(8,128)S(1)} %copy-done.3, f32[2,16,128,128]{3,2,1,0:T(8,128)S(1)} %copy-done.4, f32[2,7,16,128,128]{4,3,2,0,1:T(8,128)} %constant_dynamic-update-slice_fusion.12, f32[2,7,16,128,128]{4,3,2,1,0:T(8,128)} %bitcast.190, pred[2,7,16]{1,2,0:T(8,128)(4,1)S(1)} %copy.43, ...), kind=kOutput, calls=%fused_computation.49 | convolution fusion | flops 5645533184 | bytes 35668456 | tf_op jit(solution)/shard_map/lksij,lksjn->lsin/dot_general | solution.py:63
  267.5 31.1 %all_to_all.33 = f32[2,16,128,128]{3,2,0,1:T(8,128)S(1)} all-to-all(f32[2,16,128,128]{3,2,0,1:T(8,128)S(1)} %copy.52), channel_id=1, replica_groups=mesh['blk'=64,'states'=4] {'states'}, dimensions={1} | all-to-all | bytes 4194304 | tf_op jit(solution)/shard_map/all_to_all | solution.py:110
  300.0 4.5 fusion.11
  304.6 46.5 %all-reduce.4.cloned.1.call-done = f32[512,512]{0,1:T(8,128)} async-done(((f32[512,512]{0,1:T(8,128)}), f32[512,512]{0,1:T(8,128)}) %all-reduce.4.cloned.1.call-update) | async-done | bytes 1048592 | tf_op jit(solution)/shard_map/psum | solution.py:115
  355.6 599.0 %all-reduce.6.cloned.1.call-done = f32[512,512]{0,1:T(8,128)} async-done(((f32[512,512]{0,1:T(8,128)}), f32[512,512]{0,1:T(8,128)}) %all-reduce.6.cloned.1.call-update) | async-done | bytes 1048592 | tf_op jit(solution)/shard_map/psum | solution.py:116
  959.7 11.7 %cholesky.104 = f32[128,128]{1,0:T(8,128)S(1)} custom-call(f32[128,128]{1,0:T(8,128)S(1)} %cholesky.266), custom_call_target="Cholesky" | custom-call | tf_op jit(solution)/shard_map/jit(cholesky)/cholesky | solution.py:117
  971.6 9.8 custom-call.31
  983.9 11.7 %cholesky.217 = f32[128,128]{1,0:T(8,128)S(1)} custom-call(f32[128,128]{1,0:T(8,128)S(1)} %cholesky.270), custom_call_target="Cholesky" | custom-call | tf_op jit(solution)/shard_map/jit(cholesky)/cholesky | solution.py:117
  995.6 10.0 custom-call.32
  1007.2 11.7 %cholesky.238 = f32[128,128]{1,0:T(8,128)S(1)} custom-call(f32[128,128]{1,0:T(8,128)S(1)} %cholesky.275), custom_call_target="Cholesky" | custom-call | tf_op jit(solution)/shard_map/jit(cholesky)/cholesky | solution.py:117
  1018.9 9.8 custom-call.33
  1030.2 11.7 %cholesky.255 = f32[128,128]{1,0:T(8,128)S(1)} custom-call(f32[128,128]{1,0:T(8,128)S(1)} %convolution_subtract_fusion.5), custom_call_target="Cholesky" | custom-call | tf_op jit(solution)/shard_map/jit(cholesky)/cholesky | solution.py:117
  1047.8 14.1 %while.1 = (s32[]{:T(128)}, f32[512,512]{1,0:T(8,128)}, s32[4,2]{0,1:T(2,128)S(1)}, f32[4,128,128]{2,1,0:T(8,128)}, s32[]{:T(128)}) while((s32[]{:T(128)}, f32[512,512]{1,0:T(8,128)}, s32[4,2]{0,1:T(2,128)S(1)}, f32[4,128,128]{2,1,0:T(8,128)}, s32[]{:T(128)}) %tuple.46), condition=%wide.while_cond, body=%wide.while_body.sunk | while | flops 2 | bytes 132205 | solution.py:119
  1048.5 2.9 bitcast_dynamic-update-slice_fusion.5
  1052.0 2.9 bitcast_dynamic-update-slice_fusion.5
  1055.6 2.9 bitcast_dynamic-update-slice_fusion.5
  1061.9 40.1 %custom-call.34 = f32[4,128,128]{1,2,0:T(8,128)S(1)} custom-call(f32[4,128,128]{2,1,0:T(8,128)} %get-tuple-element.12), custom_call_target="InvertDiagBlocksLowerTriangular" | custom-call | tf_op jit(solution)/shard_map/jit(_solve_triangular)/triangular_solve | solution.py:119
  1108.7 4.8 fusion.30
  (186 shorter events, 98.6 us)
Async XLA Ops:
  8.1 6.2 copy-start.21
  8.1 8.3 copy-start.20
  8.1 23.5 %copy-start.1 = (f32[2,16,128,128]{3,2,1,0:T(8,128)S(1)}, f32[2,16,128,128]{3,2,1,0:T(8,128)}, u32[]{:S(2)}) copy-start(f32[2,16,128,128]{3,2,1,0:T(8,128)} %param.6) | copy-start | bytes 6291460
  18.6 43.7 %all-to-all-start = ((f32[64,1,1]{2,1,0:T(1,128)}), f32[64,1,1]{2,1,0:T(1,128)S(1)}, u32[]{:S(2)}, u32[]{:S(2)}) async-start(f32[64,1,1]{2,1,0:T(1,128)} %broadcast_in_dim.49), calls=%async_computation | async-start | bytes 65536 | tf_op jit(solution)/shard_map/all_to_all | solution.py:25
  33.1 57.2 %collective-permute-start.1 = (f32[1,16,128,128]{3,2,1,0:T(8,128)}, f32[1,16,128,128]{3,2,1,0:T(8,128)}, u32[]{:S(2)}, u32[]{:S(2)}) collective-permute-start(f32[1,16,128,128]{3,2,1,0:T(8,128)} %get-tuple-element.37), channel_id=1, source_target_pairs={{4,0},{8,4},{12,8},{16,12},{20,16},{24,20},{28,24},{32,28},{36,32}... | collective-permute-start | bytes 3145736 | tf_op jit(solution)/shard_map/ppermute | solution.py:18
  35.8 1.5 copy-start.22
  35.8 54.5 %collective-permute-start = (f32[1,16,128,128]{3,2,1,0:T(8,128)}, f32[1,16,128,128]{3,2,1,0:T(8,128)}, u32[]{:S(2)}, u32[]{:S(2)}) collective-permute-start(f32[1,16,128,128]{3,2,1,0:T(8,128)} %get-tuple-element.38), channel_id=1, source_target_pairs={{0,4},{4,8},{8,12},{12,16},{16,20},{20,24},{24,28},{28,32},{32,36}... | collective-permute-start | bytes 3145736 | tf_op jit(solution)/shard_map/ppermute | solution.py:17
  45.8 3.3 copy-start.6
  49.1 2.3 copy-start.7
  51.4 2.3 copy-start.8
  53.8 1.7 copy-start
  63.5 21.4 %all-to-all-start.1 = ((f32[64,1,1]{2,1,0:T(1,128)}), f32[64,1,1]{2,1,0:T(1,128)S(1)}, u32[]{:S(2)}, u32[]{:S(2)}) async-start(f32[64,1,1]{2,1,0:T(1,128)} %broadcast_in_dim.50), calls=%async_computation.1 | async-start | bytes 65536 | tf_op jit(solution)/shard_map/all_to_all | solution.py:25
  75.5 275.6 %all-reduce.4.cloned.1.call-start = ((), (), s32[]{:S(2)}) async-start(), calls=%async_computation.3 | async-start | bytes 2097152 | tf_op jit(solution)/shard_map/psum | solution.py:115
  131.9 26.2 %collective-permute-start.3 = (f32[1,16,128,128]{3,2,1,0:T(8,128)}, f32[1,16,128,128]{3,2,1,0:T(8,128)}, u32[]{:S(2)}, u32[]{:S(2)}) collective-permute-start(f32[1,16,128,128]{3,2,1,0:T(8,128)} %get-tuple-element.33), channel_id=1, source_target_pairs={{4,0},{8,4},{12,8},{16,12},{20,16},{24,20},{28,24},{32,28},{36,32}... | collective-permute-start | bytes 3145736 | tf_op jit(solution)/shard_map/ppermute | solution.py:18
  133.5 24.7 %collective-permute-start.2 = (f32[1,16,128,128]{3,2,1,0:T(8,128)S(1)}, f32[1,16,128,128]{3,2,1,0:T(8,128)}, u32[]{:S(2)}, u32[]{:S(2)}) collective-permute-start(f32[1,16,128,128]{3,2,1,0:T(8,128)S(1)} %get-tuple-element.34), channel_id=1, source_target_pairs={{0,4},{4,8},{8,12},{12,16},{16,20},{20,24},{24,28},{28,32},{32,36}... | collective-permute-start | bytes 3145736 | tf_op jit(solution)/shard_map/ppermute | solution.py:17
  148.6 3.3 copy-start.14
  151.9 2.3 copy-start.13
  154.2 2.3 copy-start.10
  156.6 2.3 copy-start.2
  170.1 3.3 copy-start.16
  196.6 7.2 copy-start.23
  196.6 7.2 copy-start.4
  199.8 23.4 %collective-permute-start.5 = (f32[1,16,128,128]{3,2,1,0:T(8,128)}, f32[1,16,128,128]{3,2,1,0:T(8,128)}, u32[]{:S(2)}, u32[]{:S(2)}) collective-permute-start(f32[1,16,128,128]{3,2,1,0:T(8,128)} %get-tuple-element.29), channel_id=1, source_target_pairs={{4,0},{8,4},{12,8},{16,12},{20,16},{24,20},{28,24},{32,28},{36,32}... | collective-permute-start | bytes 3145736 | tf_op jit(solution)/shard_map/ppermute | solution.py:18
  203.6 24.1 %collective-permute-start.4 = (f32[1,16,128,128]{3,2,1,0:T(8,128)}, f32[1,16,128,128]{3,2,1,0:T(8,128)}, u32[]{:S(2)}, u32[]{:S(2)}) collective-permute-start(f32[1,16,128,128]{3,2,1,0:T(8,128)} %get-tuple-element.30), channel_id=1, source_target_pairs={{0,4},{4,8},{8,12},{12,16},{16,20},{20,24},{24,28},{28,32},{32,36}... | collective-permute-start | bytes 3145736 | tf_op jit(solution)/shard_map/ppermute | solution.py:17
  211.9 3.3 copy-start.12
  215.2 2.3 copy-start.11
  217.6 2.3 copy-start.9
  238.9 3.3 copy-start.15
  242.2 2.3 copy-start.3
  300.0 4.5 copy-start.5
  304.6 650.0 %all-reduce.6.cloned.1.call-start = ((), (), s32[]{:S(2)}) async-start(), calls=%async_computation.4 | async-start | bytes 2097152 | tf_op jit(solution)/shard_map/psum | solution.py:116
  954.6 2.6 copy-start.17
  958.7 1.0 copy-start.19
  1047.8 57.2 %copy-start.18 = (f32[512,512]{1,0:T(8,128)S(1)}, f32[512,512]{1,0:T(8,128)}, u32[]{:S(2)}) copy-start(f32[512,512]{1,0:T(8,128)} %fusion.46) | copy-start | bytes 3145732
Sparse Core Ops, SparseCore 0:
  304.7 46.4 all-reduce.3
  353.8 600.8 all-reduce.5
